TPU v7x, 256 devices: a whole 4x4x8 slice. The times are simulated.
256 devices in a mesh: dst: 32 (over y, z), src: 8 (over x, core).
Axes of the slice: x: 4, y: 4, z: 8, core: 2. Of those that a mesh axis runs over, the one named last changes fastest.
Arguments:
- transitions: bfloat16 [16384, 128, 128], P(('dst', 'src')), may hold values from 0.0009994507 to 1
- row_block: int32 [16384], P(('dst', 'src')), may hold values from -1 to 1023, as said below
- col_block: int32 [16384], P(('dst', 'src')), may hold values from -1 to 1023, as said below
- beta_last: float32 [32, 128, 8, 128], P(None, 'dst', 'src'), may hold values from 0.2 to 2
- emissions: bfloat16 [2, 32, 128, 8, 128], P(None, None, 'dst', 'src'), may hold values from 0.019897461 to 1
- forward: bfloat16 [2, 32, 128, 8, 128], P(None, None, 'dst', 'src'), may hold values from 0.03 to 125, as said below
Outputs:
- counts: bfloat16 [16384, 128, 128], P(('dst', 'src'))
- beta_first: float32 [32, 128, 8, 128], P(None, 'dst', 'src')
- log_norms: float32 [2, 32], replicated
Inputs may be any that keep to these rules, and one draw needn't show every extreme that they name: `row_block`: slots are grouped by device (index dst * 8 + src), 64 to a device. A live slot holds a block whose source block number r has r % 8 equal to the device's src index and whose destination block lies in the device's dst index's own consecutive equal share of blocks; no block appears twice; live slots come first, and empty ones hold -1 in both arrays. One device has all 64 slots live; each device has at least one. `col_block`: same slots as row_block; -1 exactly where row_block is -1. `forward`: Positive.
All inputs are finite; a program needn't handle non-finite values.
Results may differ from a plain program's by a relative error of at most 0.0029.
Values may be sent and summed in bfloat16 or wider, within the bound.
No kernel may reach another device: no remote copies, remote signals or barrier semaphores. Data moves between devices by JAX's collectives and lax.ppermute only.
A program may use at most 64 MiB of HBM per device.

v0:
```python
import jax
import jax.numpy as jnp
from jax import lax
from jax.sharding import PartitionSpec as P

S = 131072
STEPS = 2


def body(transitions, row_block, col_block, beta_last, emissions, forward):
    source_count = lax.axis_size("src")
    seq_count = beta_last.shape[0]
    local_rows = beta_last.shape[1]
    block_size = beta_last.shape[3]
    slot_count = transitions.shape[0]
    column_count = local_rows * source_count
    total_rows = local_rows * lax.axis_size("dst")
    living = row_block >= 0
    live_float = living.astype(jnp.float32)
    row_local = jnp.where(living, row_block // source_count, 0)
    col_local = jnp.where(living, col_block % column_count, 0)
    beta_piece = beta_last[:, :, 0, :]
    count_sum = jnp.zeros((slot_count, block_size, block_size), jnp.float32)
    log_list = []
    for step_index in range(STEPS):
        emitted = emissions[step_index][:, :, 0, :]
        message = (emitted.astype(jnp.float32) * beta_piece).astype(jnp.bfloat16)
        columns = lax.all_gather(message[:, :, None, :], "src", axis=2, tiled=True)
        columns = columns.reshape(seq_count, column_count, block_size)
        alpha_rows = lax.all_gather(forward[step_index], "dst", axis=1, tiled=True)
        alpha_rows = alpha_rows.reshape(seq_count, total_rows, block_size)
        alpha_picked = jnp.take(alpha_rows, row_local, axis=1)
        picked = jnp.take(columns, col_local, axis=1)
        products = jnp.einsum(
            "bcj,cij->cbi", picked, transitions, preferred_element_type=jnp.float32
        )
        products = products * live_float[:, None, None]
        partial_value = jax.ops.segment_sum(products, row_local, num_segments=total_rows)
        raw_sums = lax.psum_scatter(partial_value, "dst", scatter_dimension=0, tiled=True)
        own_alpha = forward[step_index][:, :, 0, :]
        local_term = jnp.einsum(
            "kbr,bkr->b", raw_sums, own_alpha, preferred_element_type=jnp.float32
        )
        scale_now = lax.psum(local_term, ("dst", "src")) / S
        beta_piece = jnp.transpose(raw_sums / scale_now[None, :, None], (1, 0, 2))
        scaled = (columns.astype(jnp.float32) / scale_now[:, None, None]).astype(jnp.bfloat16)
        scaled_picked = jnp.take(scaled, col_local, axis=1)
        count_sum = count_sum + jnp.einsum(
            "bci,bcj->cij", alpha_picked, scaled_picked, preferred_element_type=jnp.float32
        )
        log_list.append(jnp.log(scale_now))
    counts = (count_sum * transitions.astype(jnp.float32) * live_float[:, None, None]).astype(
        jnp.bfloat16
    )
    return (counts, beta_piece[:, :, None, :], jnp.stack(log_list))


def solution(mesh):
    return jax.shard_map(
        body,
        mesh=mesh,
        in_specs=(
            P(("dst", "src"), None, None),
            P(("dst", "src")),
            P(("dst", "src")),
            P(None, "dst", "src", None),
            P(None, None, "dst", "src", None),
            P(None, None, "dst", "src", None),
        ),
        out_specs=(P(("dst", "src"), None, None), P(None, "dst", "src", None), P()),
        check_vma=False,
    )
```

profile of v0, /device:TPU:1, one launch (start us, length us, event | category | flops | bytes accessed | tf_op | source)
XLA Modules:
  0.0 728.8 jit_solution(5440016924613923832)
XLA Ops:
  7.2 0.8 compare_and_fusion
  8.1 0.8 fusion.35
  8.9 0.9 fusion.24
  9.7 15.9 %all_gather.13 = bf16[32,4,8,128]{3,0,1,2:T(8,128)(2,1)S(1)} all-gather(bf16[32,4,1,128]{3,0,1,2:T(8,128)(2,1)S(1)} %fusion.24), channel_id=1, replica_groups=mesh['dst'=32,'src'=8] {'src'}, dimensions={2}, use_global_device_ids=true | all-gather | bytes 294912 | tf_op jit(solution)/shard_map/all_gather | solution.py:28
  25.9 1.4 gather_fusion.1
  27.3 2.3 convolution_multiply_fusion.1
  29.6 1.6 broadcast.28.clone
  31.2 8.0 %scatter_fusion = f32[128,32,128]{2,1,0:T(8,128)} fusion(f32[128,32,128]{2,1,0:T(8,128)} %broadcast.28.clone, s32[64]{0:T(128)S(1)} %get-tuple-element.28, f32[64,32,128]{2,1,0:T(8,128)S(1)} %convolution_multiply_fusion.1), kind=kCustom, calls=%fused_computation.6 | custom fusion | flops 262144 | bytes 3145984 | tf_op jit(solution)/shard_map/scatter-add | solution.py:38
  39.4 0.6 copy.54
  40.1 0.6 copy.52
  40.8 213.9 %reduce-scatter.3.cloned.1.call-done = f32[4,32,128]{2,1,0:T(8,128)} async-done(((f32[128,32,128]{2,1,0:T(8,128)}), f32[4,32,128]{2,1,0:T(8,128)}) %reduce-scatter.3.cloned.1.call-update) | async-done | bytes 65552 | tf_op jit(solution)/shard_map/reduce_scatter | solution.py:39
  254.7 1.0 multiply_reduce_fusion.1
  255.7 79.9 %psum.14 = f32[32]{0:T(128)S(1)} all-reduce(f32[32]{0:T(128)S(1)} %multiply_reduce_fusion.1), channel_id=1, replica_groups=mesh['dst'=32,'src'=8] {'dst','src'}, use_global_device_ids=true, to_apply=%region_2.5 | all-reduce | flops 32 | bytes 256 | tf_op jit(solution)/shard_map/psum | solution.py:44
  335.6 0.9 fusion.23
  336.5 12.6 %all-gather.2 = bf16[32,4,1024]{2,0,1:T(8,128)(2,1)S(1)} all-gather(bf16[32,4,128]{2,0,1:T(8,128)(2,1)S(1)} %fusion.23), channel_id=4, replica_groups=mesh['dst'=32,'src'=8] {'src'}, dimensions={2}, use_global_device_ids=true | all-gather | bytes 294912 | tf_op jit(solution)/shard_map/all_gather | solution.py:28
  349.5 0.6 copy-done.1
  350.1 1.4 gather_fusion.4
  351.6 2.3 convolution_multiply_fusion
  353.8 1.6 broadcast.28
  355.4 8.0 %scatter_fusion.1 = f32[128,32,128]{2,1,0:T(8,128)} fusion(f32[128,32,128]{2,1,0:T(8,128)} %broadcast.28, s32[64]{0:T(128)S(1)} %copy-done.6, f32[64,32,128]{2,1,0:T(8,128)S(1)} %convolution_multiply_fusion), kind=kCustom, calls=%fused_computation.7 | custom fusion | flops 262144 | bytes 3145984 | tf_op jit(solution)/shard_map/scatter-add | solution.py:38
  363.6 1.9 gather_fusion.3
  365.5 43.8 %all-gather.6.cloned.1.call-done = bf16[1,32,128,1,128]{4,1,3,0,2:T(8,128)(2,1)} async-done(((bf16[1,32,4,1,128]{4,1,3,0,2:T(8,128)(2,1)}), bf16[1,32,128,1,128]{4,1,3,0,2:T(8,128)(2,1)}) %all-gather.6.cloned.1.call-update) | async-done | bytes 1048592 | tf_op jit(solution)/shard_map/all_gather | solution.py:30
  409.3 2.6 gather_fusion
  412.0 1.4 gather_fusion.2
  413.5 216.1 %reduce-scatter.5.cloned.1.call-done = f32[4,32,128]{2,1,0:T(8,128)} async-done(((f32[128,32,128]{2,1,0:T(8,128)}), f32[4,32,128]{2,1,0:T(8,128)}) %reduce-scatter.5.cloned.1.call-update) | async-done | bytes 65552 | tf_op jit(solution)/shard_map/reduce_scatter | solution.py:39
  629.6 1.0 multiply_reduce_fusion
  630.6 4.1 fusion.3
  634.7 79.6 %psum.15 = f32[32]{0:T(128)S(1)} all-reduce(f32[32]{0:T(128)S(1)} %multiply_reduce_fusion), channel_id=1, replica_groups=mesh['dst'=32,'src'=8] {'dst','src'}, use_global_device_ids=true, to_apply=%region_5.8 | all-reduce | flops 32 | bytes 256 | tf_op jit(solution)/shard_map/psum | solution.py:44
  714.5 0.7 copy.41
  715.2 1.4 gather_fusion.5
  716.6 0.6 pad_maximum_fusion
  717.2 5.0 multiply_convert_fusion
  (36 shorter events, 1.4 us)
Async XLA Ops:
  7.2 20.2 %copy-start = (bf16[64,128,128]{2,1,0:T(8,128)(2,1)S(1)}, bf16[64,128,128]{2,1,0:T(8,128)(2,1)}, u32[]{:S(2)}) copy-start(bf16[64,128,128]{2,1,0:T(8,128)(2,1)} %param.10) | copy-start | bytes 6291460
  7.2 247.6 %reduce-scatter.3.cloned.1.call-start = ((), (), s32[]{:S(2)}) async-start(), calls=%async_computation.2 | async-start | bytes 2162688 | tf_op jit(solution)/shard_map/reduce_scatter | solution.py:39
  8.1 23.1 %copy-start.5 = (s32[64]{0:T(128)}, s32[64]{0:T(128)S(1)}, u32[]{:S(2)}) copy-start(s32[64]{0:T(128)S(1)} %get-tuple-element.28) | copy-start | bytes 772
  31.2 8.1 %copy-start.4 = (bf16[2,32,4,1,128]{4,2,3,1,0:T(4,128)(2,1)S(1)}, bf16[2,32,4,1,128]{4,2,3,1,0:T(4,128)(2,1)}, u32[]{:S(2)}) copy-start(bf16[2,32,4,1,128]{4,2,3,1,0:T(4,128)(2,1)} %param.15) | copy-start | bytes 196612
  39.3 324.3 %all-gather.8.cloned.1.call-start = ((), (), s32[]{:S(2)}) async-start(), calls=%async_computation.5 | async-start | bytes 1081344 | tf_op jit(solution)/shard_map/all_gather | solution.py:30
  40.0 369.3 %all-gather.6.cloned.1.call-start = ((), (), s32[]{:S(2)}) async-start(), calls=%async_computation.4 | async-start | bytes 1081344 | tf_op jit(solution)/shard_map/all_gather | solution.py:30
  40.8 588.9 %reduce-scatter.5.cloned.1.call-start = ((), (), s32[]{:S(2)}) async-start(), calls=%async_computation.3 | async-start | bytes 2162688 | tf_op jit(solution)/shard_map/reduce_scatter | solution.py:39
  349.4 0.7 copy-start.1
  351.6 3.9 copy-start.6
  630.6 83.8 %copy-start.2 = (bf16[32,32,128]{2,1,0:T(8,128)(2,1)S(1)}, bf16[32,32,128]{2,1,0:T(8,128)(2,1)}, u32[]{:S(2)}) copy-start(bf16[32,32,128]{2,1,0:T(8,128)(2,1)} %copy-done.1) | copy-start | bytes 786436
  630.6 83.9 %copy-start.3 = (f32[4,32,128]{2,1,0:T(8,128)S(1)}, f32[4,32,128]{2,1,0:T(8,128)}, u32[]{:S(2)}) copy-start(f32[4,32,128]{2,1,0:T(8,128)} %reduce-scatter.5.cloned.1.call-done) | copy-start | bytes 196612
Sparse Core Ops, SparseCore 0:
  39.4 215.2 reduce-scatter.2
  257.3 74.8 all-gather.7
  335.4 73.8 all-gather.5
  413.5 216.0 reduce-scatter.4
where the time goes:
time: 730 us; the launch traced here: 729 us
  waiting for transfers between devices  474 us (65%)
  blocking collectives  188 us (26%)
  other arithmetic  21.5 us (3%)
  local copies, waits for them, and re-layouts  17.5 us (2%)
  between operations  13.9 us (2%)
  matrix products  13.7 us (2%)
    reduce_scatter x2, waiting for transfers between devices, body(): lax.psum_scatter(partial_value, 'dst', scatter_dimension=0, tiled=True)  430 us
    psum x2, blocking collectives, body(): scale_now = lax.psum(local_term, ('dst', 'src')) / S  160 us
    all_gather x2, waiting for transfers between devices, body(): alpha_rows = lax.all_gather(forward[step_index], 'dst', axis=1, tiled=True)  43.8 us
    all_gather x2, blocking collectives, body(): columns = lax.all_gather(message[:, :, None, :], 'src', axis=2, tiled=True)  28.5 us
    scatter-add x2, other arithmetic, body(): jax.ops.segment_sum(products, row_local, num_segments=total_rows)  16.1 us
  transfers between devices with their start and end apart: 4, of which 3 were waited for; matrix products, arithmetic and copies ran while one was open for 3% of the time, Pallas kernels for 0%

commit v1 on v0

--- a/solution.py
+++ b/solution.py
@@ -27,7 +27,10 @@
         message = (emitted.astype(jnp.float32) * beta_piece).astype(jnp.bfloat16)
         columns = lax.all_gather(message[:, :, None, :], "src", axis=2, tiled=True)
         columns = columns.reshape(seq_count, column_count, block_size)
-        alpha_rows = lax.all_gather(forward[step_index], "dst", axis=1, tiled=True)
+        alpha_rows = jnp.concatenate(
+            lax.all_to_all(jnp.stack([forward[step_index]] * lax.axis_size("dst")), "dst", 0, 0),
+            axis=1,
+        )
         alpha_rows = alpha_rows.reshape(seq_count, total_rows, block_size)
         alpha_picked = jnp.take(alpha_rows, row_local, axis=1)
         picked = jnp.take(columns, col_local, axis=1)

time: 730 us -> 690 us (0.945)
  waiting for transfers between devices: 474 us -> 416 us
  starting transfers between devices: 0.16 us -> 15.1 us
    all_gather x2 -> x0, waiting for transfers between devices: 43.8 us -> none  [body(): alpha_rows = lax.all_gather(forward[step_index], 'dst', axis=1, tiled=True)]
    reduce_scatter x2, waiting for transfers between devices: 430 us -> 388 us  [body(): lax.psum_scatter(partial_value, 'dst', scatter_dimension=0, tiled=True)]
    all_to_all x0 -> x2, waiting for transfers between devices: none -> 27.7 us  [body(): lax.all_to_all(jnp.stack([forward[step_index]] * lax.axis_size('dst')), '...]
    all_to_all x0 -> x2, starting transfers between devices: none -> 15 us  [body(): lax.all_to_all(jnp.stack([forward[step_index]] * lax.axis_size('dst')), '...]
where the time goes in v1:
time: 690 us; the launch traced here: 688 us
  waiting for transfers between devices  416 us (60%)
  blocking collectives  191 us (28%)
  other arithmetic  21.7 us (3%)
  local copies, waits for them, and re-layouts  17.6 us (3%)
  starting transfers between devices  15.1 us (2%)
  between operations  14.2 us (2%)
  matrix products  13.5 us (2%)
    reduce_scatter x2, waiting for transfers between devices, body(): lax.psum_scatter(partial_value, 'dst', scatter_dimension=0, tiled=True)  388 us
    psum x2, blocking collectives, body(): scale_now = lax.psum(local_term, ('dst', 'src')) / S  163 us
    all_gather x2, blocking collectives, body(): columns = lax.all_gather(message[:, :, None, :], 'src', axis=2, tiled=True)  27.9 us
    all_to_all x2, waiting for transfers between devices, body(): lax.all_to_all(jnp.stack([forward[step_index]] * lax.axis_size('dst')), '...  27.7 us
    scatter-add x2, other arithmetic, body(): jax.ops.segment_sum(products, row_local, num_segments=total_rows)  16.1 us
    all_to_all x2, starting transfers between devices, body(): lax.all_to_all(jnp.stack([forward[step_index]] * lax.axis_size('dst')), '...  15 us
  transfers between devices with their start and end apart: 4, of which 3 were waited for; matrix products, arithmetic and copies ran while one was open for 3% of the time, Pallas kernels for 0%

profile of v1, /device:TPU:1, one launch (start us, length us, event | category | flops | bytes accessed | tf_op | source)
XLA Modules:
  0.0 688.2 jit_solution(1062422283150931931)
XLA Ops:
  7.2 0.8 compare_and_fusion
  8.1 0.8 fusion.34
  8.9 0.9 fusion.24
  9.7 15.9 %all_gather.6 = bf16[32,4,8,128]{3,0,1,2:T(8,128)(2,1)S(1)} all-gather(bf16[32,4,1,128]{3,0,1,2:T(8,128)(2,1)S(1)} %fusion.24), channel_id=1, replica_groups=mesh['dst'=32,'src'=8] {'src'}, dimensions={2}, use_global_device_ids=true | all-gather | bytes 294912 | tf_op jit(solution)/shard_map/all_gather | solution.py:28
  25.9 1.4 gather_fusion.1
  27.3 2.3 convolution_multiply_fusion.1
  29.6 1.6 broadcast.32.clone
  31.2 8.0 %scatter_fusion = f32[128,32,128]{2,1,0:T(8,128)} fusion(f32[128,32,128]{2,1,0:T(8,128)} %broadcast.32.clone, s32[64]{0:T(128)S(1)} %get-tuple-element.28, f32[64,32,128]{2,1,0:T(8,128)S(1)} %convolution_multiply_fusion.1), kind=kCustom, calls=%fused_computation.6 | custom fusion | flops 262144 | bytes 3145984 | tf_op jit(solution)/shard_map/scatter-add | solution.py:41
  39.3 215.4 %reduce-scatter.3.cloned.1.call-done = f32[4,32,128]{2,1,0:T(8,128)} async-done(((f32[128,32,128]{2,1,0:T(8,128)}), f32[4,32,128]{2,1,0:T(8,128)}) %reduce-scatter.3.cloned.1.call-update) | async-done | bytes 65552 | tf_op jit(solution)/shard_map/reduce_scatter | solution.py:42
  254.7 1.2 multiply_reduce_fusion.1
  256.0 1.3 stack.15
  257.2 6.7 all-to-all-start
  263.9 83.0 %psum.14 = f32[32]{0:T(128)S(1)} all-reduce(f32[32]{0:T(128)S(1)} %multiply_reduce_fusion.1), channel_id=1, replica_groups=mesh['dst'=32,'src'=8] {'dst','src'}, use_global_device_ids=true, to_apply=%region_2.5 | all-reduce | flops 32 | bytes 256 | tf_op jit(solution)/shard_map/psum | solution.py:47
  347.5 12.0 %all-gather = bf16[32,4,1024]{2,0,1:T(8,128)(2,1)S(1)} all-gather(bf16[32,4,128]{2,0,1:T(8,128)(2,1)S(1)} %fusion.23), channel_id=2, replica_groups=mesh['dst'=32,'src'=8] {'src'}, dimensions={2}, use_global_device_ids=true | all-gather | bytes 294912 | tf_op jit(solution)/shard_map/all_gather | solution.py:28
  360.0 0.6 copy-done.1
  360.6 1.4 gather_fusion.4
  362.0 2.3 convolution_multiply_fusion
  364.3 1.6 broadcast.32
  365.9 8.0 %scatter_fusion.1 = f32[128,32,128]{2,1,0:T(8,128)} fusion(f32[128,32,128]{2,1,0:T(8,128)} %broadcast.32, s32[64]{0:T(128)S(1)} %copy-done.8, f32[64,32,128]{2,1,0:T(8,128)S(1)} %convolution_multiply_fusion), kind=kCustom, calls=%fused_computation.7 | custom fusion | flops 262144 | bytes 3145984 | tf_op jit(solution)/shard_map/scatter-add | solution.py:41
  373.9 1.3 stack.16
  375.2 8.4 %all-to-all-start.1 = ((bf16[32,32,4,1,128]{4,1,2,3,0:T(8,128)(2,1)}), bf16[32,32,4,1,128]{4,1,2,3,0:T(8,128)(2,1)S(1)}, u32[]{:S(2)}, u32[]{:S(2)}) async-start(bf16[32,32,4,1,128]{4,1,2,3,0:T(8,128)(2,1)} %stack.16), calls=%async_computation.2 | async-start | bytes 2097152 | tf_op jit(solution)/shard_map/all_to_all | solution.py:31
  383.6 2.7 gather_fusion
  386.3 27.7 %all-to-all-done.1 = bf16[32,32,4,1,128]{4,1,2,3,0:T(8,128)(2,1)S(1)} async-done(((bf16[32,32,4,1,128]{4,1,2,3,0:T(8,128)(2,1)}), bf16[32,32,4,1,128]{4,1,2,3,0:T(8,128)(2,1)S(1)}, u32[]{:S(2)}, u32[]{:S(2)}) %all-to-all-start.1) | async-done | bytes 1048608 | tf_op jit(solution)/shard_map/all_to_all | solution.py:31
  414.0 1.4 gather_fusion.3
  415.6 0.7 gather_fusion.2
  416.2 172.4 %reduce-scatter.5.cloned.1.call-done = f32[4,32,128]{2,1,0:T(8,128)} async-done(((f32[128,32,128]{2,1,0:T(8,128)}), f32[4,32,128]{2,1,0:T(8,128)}) %reduce-scatter.5.cloned.1.call-update) | async-done | bytes 65552 | tf_op jit(solution)/shard_map/reduce_scatter | solution.py:42
  588.6 1.2 multiply_reduce_fusion
  589.8 3.9 fusion.3
  593.7 79.7 %psum.15 = f32[32]{0:T(128)S(1)} all-reduce(f32[32]{0:T(128)S(1)} %multiply_reduce_fusion), channel_id=1, replica_groups=mesh['dst'=32,'src'=8] {'dst','src'}, use_global_device_ids=true, to_apply=%region_5.8 | all-reduce | flops 32 | bytes 256 | tf_op jit(solution)/shard_map/psum | solution.py:47
  673.6 0.7 copy.41
  674.3 1.4 gather_fusion.5
  676.3 5.0 multiply_convert_fusion
  (46 shorter events, 2.4 us)
Async XLA Ops:
  7.2 20.2 %copy-start = (bf16[64,128,128]{2,1,0:T(8,128)(2,1)S(1)}, bf16[64,128,128]{2,1,0:T(8,128)(2,1)}, u32[]{:S(2)}) copy-start(bf16[64,128,128]{2,1,0:T(8,128)(2,1)} %param.10) | copy-start | bytes 6291460
  7.2 247.5 %reduce-scatter.3.cloned.1.call-start = ((), (), s32[]{:S(2)}) async-start(), calls=%async_computation.4 | async-start | bytes 2162688 | tf_op jit(solution)/shard_map/reduce_scatter | solution.py:42
  8.1 23.1 %copy-start.7 = (s32[64]{0:T(128)}, s32[64]{0:T(128)S(1)}, u32[]{:S(2)}) copy-start(s32[64]{0:T(128)S(1)} %get-tuple-element.28) | copy-start | bytes 772
  31.2 8.1 %copy-start.4 = (bf16[2,32,4,1,128]{4,2,3,1,0:T(4,128)(2,1)S(1)}, bf16[2,32,4,1,128]{4,2,3,1,0:T(4,128)(2,1)}, u32[]{:S(2)}) copy-start(bf16[2,32,4,1,128]{4,2,3,1,0:T(4,128)(2,1)} %param.15) | copy-start | bytes 196612
  254.7 92.7 %copy-start.6 = (f32[4,32,128]{2,1,0:T(8,128)S(1)}, f32[4,32,128]{2,1,0:T(8,128)}, u32[]{:S(2)}) copy-start(f32[4,32,128]{2,1,0:T(8,128)} %reduce-scatter.3.cloned.1.call-done) | copy-start | bytes 196612
  257.2 116.7 %all-to-all-start = ((bf16[32,32,4,1,128]{4,1,2,3,0:T(8,128)(2,1)}), bf16[32,32,4,1,128]{4,1,2,3,0:T(8,128)(2,1)}, u32[]{:S(2)}, u32[]{:S(2)}) async-start(bf16[32,32,4,1,128]{4,1,2,3,0:T(8,128)(2,1)} %stack.15), calls=%async_computation | async-start | bytes 2097152 | tf_op jit(solution)/shard_map/all_to_all | solution.py:31
  263.9 324.7 %reduce-scatter.5.cloned.1.call-start = ((), (), s32[]{:S(2)}) async-start(), calls=%async_computation.5 | async-start | bytes 2162688 | tf_op jit(solution)/shard_map/reduce_scatter | solution.py:42
  347.4 12.1 %copy-start.9 = (f32[32]{0:T(128)}, f32[32]{0:T(128)S(1)}, u32[]{:S(2)}) copy-start(f32[32]{0:T(128)S(1)} %get-tuple-element.23) | copy-start | bytes 388
  359.9 0.7 copy-start.1
  362.0 3.9 copy-start.8
  375.2 40.2 %copy-start.10 = (f32[32]{0:T(128)S(1)}, f32[32]{0:T(128)}, u32[]{:S(2)}) copy-start(f32[32]{0:T(128)} %copy-done.9) | copy-start | bytes 388
  375.2 38.8 %all-to-all-start.1 = ((bf16[32,32,4,1,128]{4,1,2,3,0:T(8,128)(2,1)}), bf16[32,32,4,1,128]{4,1,2,3,0:T(8,128)(2,1)S(1)}, u32[]{:S(2)}, u32[]{:S(2)}) async-start(bf16[32,32,4,1,128]{4,1,2,3,0:T(8,128)(2,1)} %stack.16), calls=%async_computation.2 | async-start | bytes 2097152 | tf_op jit(solution)/shard_map/all_to_all | solution.py:31
  589.8 83.6 %copy-start.2 = (bf16[32,32,128]{2,1,0:T(8,128)(2,1)S(1)}, bf16[32,32,128]{2,1,0:T(8,128)(2,1)}, u32[]{:S(2)}) copy-start(bf16[32,32,128]{2,1,0:T(8,128)(2,1)} %copy-done.1) | copy-start | bytes 786436
  589.8 83.8 %copy-start.5 = (f32[4,32,128]{2,1,0:T(8,128)S(1)}, f32[4,32,128]{2,1,0:T(8,128)}, u32[]{:S(2)}) copy-start(f32[4,32,128]{2,1,0:T(8,128)} %reduce-scatter.5.cloned.1.call-done) | copy-start | bytes 196612
  589.8 86.0 %copy-start.11 = (f32[1,32]{1,0:T(1,128)S(1)}, f32[1,32]{1,0:T(1,128)}, u32[]{:S(2)}) copy-start(f32[1,32]{1,0:T(1,128)} %get-tuple-element.22) | copy-start | bytes 388
  593.7 82.6 %copy-start.3 = (bf16[64,32,128]{2,1,0:T(8,128)(2,1)S(1)}, bf16[64,32,128]{2,1,0:T(8,128)(2,1)}, u32[]{:S(2)}) copy-start(bf16[64,32,128]{2,1,0:T(8,128)(2,1)} %gather_fusion.3) | copy-start | bytes 1572868
Sparse Core Ops, SparseCore 0:
  39.4 215.2 reduce-scatter.2
  374.0 214.5 reduce-scatter.4
